TPU v7x, 32 devices: a whole 2x2x4 slice. The times are simulated.
32 devices in a mesh: row: 8 (over z, core), col: 4 (over y, x).
Axes of the slice: x: 2, y: 2, z: 4, core: 2. Of those that a mesh axis runs over, the one named last changes fastest.
Arguments:
- tokens: bfloat16 [16384, 1024], P('row', 'col'), may hold values from -6 to 6
- memory: bfloat16 [4096, 1024], P('row', 'col'), may hold values from -6 to 6
- old_memory: bfloat16 [12288, 1024], P('row', 'col'), may hold values from -6 to 6
- doc_ids: int32 [8, 4096], P('row'), may hold values from 0 to 5, as said below
- norm_gains: bfloat16 [2, 1024], P(None, 'row'), may hold values from 0.5 to 1.5
- comp_weight: bfloat16 [3072, 1024], P('row', 'col'), may hold values from -0.109375 to 0.109375
- query_weight: bfloat16 [1024, 1024], P('row', 'col'), may hold values from -0.1875 to 0.1875
- key_weight: bfloat16 [1024, 1024], P('row', 'col'), may hold values from -0.1875 to 0.1875
- value_weight: bfloat16 [1024, 1024], P('row', 'col'), may hold values from -0.1875 to 0.1875
- proj_weight: bfloat16 [1024, 1024], P('col', 'row'), may hold values from -1.5 to 1.5
- up_weight: bfloat16 [1024, 4096], P('row', 'col'), may hold values from -0.1875 to 0.1875
- down_weight: bfloat16 [4096, 1024], P('col', 'row'), may hold values from -0.09375 to 0.09375
- cotangent: bfloat16 [16384, 1024], P('row', 'col'), may hold values from -6 to 6
Outputs:
- layer_out: bfloat16 [16384, 1024], P('row', 'col')
- grad_x: float32 [16384, 1024], P('row', 'col')
- grad_gains: float32 [2, 1024], P(None, 'row')
- grad_comp: float32 [3072, 1024], P('row', 'col')
- grad_query: float32 [1024, 1024], P('row', 'col')
- grad_key: float32 [1024, 1024], P('row', 'col')
- grad_value: float32 [1024, 1024], P('row', 'col')
- grad_proj: float32 [1024, 1024], P('col', 'row')
- grad_up: float32 [1024, 4096], P('row', 'col')
- grad_down: float32 [4096, 1024], P('col', 'row')
Inputs may be any that keep to these rules, and one draw needn't show every extreme that they name: In each row of doc_ids the numbers never fall and every number occurs; every document covers 200 entries or more.
All inputs are finite; a program needn't handle non-finite values.
Results may differ from a plain program's by a relative error of at most 0.015.
Values may be sent and summed in bfloat16 or wider, within the bound.
A program may use at most 192 MiB of HBM per device.

v0:
```python
import jax
import jax.numpy as jnp
from jax import lax
from jax.sharding import PartitionSpec as P

RATE = 3
HD = 128


def normalize(rows, gain):
    centre = rows - jnp.mean(rows, axis=-1, keepdims=True)
    spread = jnp.mean(centre * centre, axis=-1, keepdims=True)
    return centre * lax.rsqrt(spread + 1e-05) * gain


def contract_rows(left, right):
    return lax.dot_general(
        left, right, (((0,), (0,)), ((), ())), preferred_element_type=jnp.float32
    )


def contract_cols(left, right):
    return lax.dot_general(
        left, right, (((1,), (1,)), ((), ())), preferred_element_type=jnp.float32
    )


def on_device(
    tokens,
    memory,
    old_memory,
    doc_ids,
    norm_gains,
    comp_weight,
    query_weight,
    key_weight,
    value_weight,
    proj_weight,
    up_weight,
    down_weight,
    cotangent,
):
    full_tokens, full_memory, full_old, full_grad = (
        lax.all_gather(tokens, "col", axis=1, tiled=True),
        lax.all_gather(memory, "col", axis=1, tiled=True),
        lax.all_gather(old_memory, "col", axis=1, tiled=True),
        lax.all_gather(cotangent, "col", axis=1, tiled=True),
    )
    comp_full, query_full, key_full, value_full, up_full = (
        lax.all_gather(comp_weight, "row", axis=0, tiled=True),
        lax.all_gather(query_weight, "row", axis=0, tiled=True),
        lax.all_gather(key_weight, "row", axis=0, tiled=True),
        lax.all_gather(value_weight, "row", axis=0, tiled=True),
        lax.all_gather(up_weight, "row", axis=0, tiled=True),
    )
    proj_full, down_full, gain_full = (
        lax.all_gather(proj_weight, "row", axis=1, tiled=True),
        lax.all_gather(down_weight, "row", axis=1, tiled=True),
        lax.all_gather(norm_gains, "row", axis=1, tiled=True),
    )
    width = full_tokens.shape[1]
    slab = tokens.shape[1]
    column = lax.axis_index("col")
    seq_len = tokens.shape[0]
    mem_len = memory.shape[0]
    comp_len = old_memory.shape[0] // RATE
    start_tok = comp_len + mem_len
    all_keys = start_tok + seq_len
    gain_one = gain_full[0].astype(jnp.float32)
    gain_two = gain_full[1].astype(jnp.float32)
    old_rows = full_old.reshape(comp_len, RATE * width)
    compressed = jnp.dot(old_rows, comp_full, preferred_element_type=jnp.float32).astype(
        jnp.bfloat16
    )
    compressed_all = lax.all_gather(compressed, "col", axis=1, tiled=True)
    stacked = jnp.concatenate([compressed_all, full_memory, full_tokens], axis=0).astype(
        jnp.float32
    )
    normed = normalize(stacked, gain_one).astype(jnp.bfloat16)
    queries = jnp.dot(normed[start_tok:], query_full, preferred_element_type=jnp.float32).astype(
        jnp.bfloat16
    )
    keys = jnp.dot(normed, key_full, preferred_element_type=jnp.float32).astype(jnp.bfloat16)
    values = jnp.dot(normed, value_full, preferred_element_type=jnp.float32).astype(jnp.bfloat16)
    local_heads = queries.shape[1] // HD
    key_heads = keys.reshape(all_keys, local_heads, HD)
    value_heads = values.reshape(all_keys, local_heads, HD)
    doc_row = doc_ids[0]
    key_doc = jnp.concatenate(
        [doc_row[RATE - 1 : RATE * comp_len : RATE], doc_row[RATE * comp_len :]]
    )
    key_place = jnp.arange(all_keys, dtype=jnp.int32) - start_tok
    query_doc = doc_row[RATE * comp_len + mem_len :]
    query_place = jnp.arange(seq_len, dtype=jnp.int32)
    block = min(512, seq_len)
    steps_count = seq_len // block
    scale = HD ** (-0.5)
    query_blocks = queries.reshape(steps_count, block, local_heads, HD)
    doc_blocks = query_doc.reshape(steps_count, block)
    place_blocks = query_place.reshape(steps_count, block)

    def masked_scores(query_block, doc_block, place_block):
        allowed = (doc_block[:, None] == key_doc[None, :]) & (
            key_place[None, :] <= place_block[:, None]
        )
        scores = (
            jnp.einsum("qhd,khd->hqk", query_block, key_heads, preferred_element_type=jnp.float32)
            * scale
        )
        return jnp.where(allowed[None], scores, -1e30)

    def forward_block(items):
        query_block, doc_block, place_block = items
        scores = masked_scores(query_block, doc_block, place_block)
        top = jnp.max(scores, axis=-1, keepdims=True)
        raw = jnp.exp(scores - top)
        total = jnp.sum(raw, axis=-1, keepdims=True)
        rounded = (raw / total).astype(jnp.bfloat16)
        mixed_block = jnp.einsum(
            "hqk,khd->qhd", rounded, value_heads, preferred_element_type=jnp.float32
        )
        return (mixed_block, top, total)

    mixed_blocks, tops, totals = lax.map(forward_block, (query_blocks, doc_blocks, place_blocks))
    mixed = mixed_blocks.reshape(seq_len, local_heads * HD).astype(jnp.bfloat16)
    branch = lax.psum(jnp.dot(mixed, proj_full, preferred_element_type=jnp.float32), "col")
    resid = full_tokens.astype(jnp.float32) + branch
    hidden_in = normalize(resid, gain_two).astype(jnp.bfloat16)
    upper = jnp.dot(hidden_in, up_full, preferred_element_type=jnp.float32)
    active = jax.nn.gelu(upper).astype(jnp.bfloat16)
    down_terms = jnp.dot(active, down_full, preferred_element_type=jnp.float32)
    final = resid + lax.psum(down_terms.astype(jnp.bfloat16), "col").astype(jnp.float32)
    layer_out = lax.dynamic_slice_in_dim(final, column * slab, slab, 1).astype(jnp.bfloat16)
    grad_down = contract_rows(active, full_grad)
    grad_active = contract_cols(full_grad, down_full)
    _, gelu_pull = jax.vjp(jax.nn.gelu, upper)
    grad_upper = gelu_pull(grad_active)[0].astype(jnp.bfloat16)
    grad_up = contract_rows(hidden_in, grad_upper)
    grad_hidden = lax.psum(contract_cols(grad_upper, up_full), "col")
    _, second_pull = jax.vjp(normalize, resid, gain_two)
    grad_resid_norm, grad_gain_two = second_pull(grad_hidden)
    grad_resid = full_grad.astype(jnp.float32) + grad_resid_norm
    grad_branch = grad_resid.astype(jnp.bfloat16)
    grad_proj = contract_rows(mixed, grad_branch)
    grad_mixed = contract_cols(grad_branch, proj_full).astype(jnp.bfloat16)
    grad_blocks = grad_mixed.reshape(steps_count, block, local_heads, HD)

    def backward_block(carry, items):
        grad_keys, grad_values = carry
        query_block, doc_block, place_block, top, total, grad_out = items
        scores = masked_scores(query_block, doc_block, place_block)
        probs = jnp.exp(scores - top) / total
        rounded = probs.astype(jnp.bfloat16)
        grad_probs = jnp.einsum(
            "qhd,khd->hqk", grad_out, value_heads, preferred_element_type=jnp.float32
        )
        grad_scores = (
            probs * (grad_probs - jnp.sum(probs * grad_probs, axis=-1, keepdims=True))
        ).astype(jnp.bfloat16)
        grad_query_block = (
            jnp.einsum("hqk,khd->qhd", grad_scores, key_heads, preferred_element_type=jnp.float32)
            * scale
        )
        grad_keys = (
            grad_keys
            + jnp.einsum(
                "hqk,qhd->khd", grad_scores, query_block, preferred_element_type=jnp.float32
            )
            * scale
        )
        grad_values = grad_values + jnp.einsum(
            "hqk,qhd->khd", rounded, grad_out, preferred_element_type=jnp.float32
        )
        return ((grad_keys, grad_values), grad_query_block)

    empty = jnp.zeros((all_keys, local_heads, HD), jnp.float32)
    (grad_key_heads, grad_value_heads), grad_query_blocks = lax.scan(
        backward_block,
        (empty, empty),
        (query_blocks, doc_blocks, place_blocks, tops, totals, grad_blocks),
    )
    grad_queries = grad_query_blocks.reshape(seq_len, local_heads * HD).astype(jnp.bfloat16)
    grad_keys_low = grad_key_heads.reshape(all_keys, local_heads * HD).astype(jnp.bfloat16)
    grad_values_low = grad_value_heads.reshape(all_keys, local_heads * HD).astype(jnp.bfloat16)
    grad_query = contract_rows(normed[start_tok:], grad_queries)
    grad_key = contract_rows(normed, grad_keys_low)
    grad_value = contract_rows(normed, grad_values_low)
    back_keys = contract_cols(grad_keys_low, key_full) + contract_cols(grad_values_low, value_full)
    back_queries = contract_cols(grad_queries, query_full)
    partial_rows = jnp.concatenate(
        [back_keys[:start_tok], back_keys[start_tok:] + back_queries], axis=0
    )
    grad_normed = lax.psum(partial_rows, "col")
    _, first_pull = jax.vjp(normalize, stacked, gain_one)
    grad_stacked, grad_gain_one = first_pull(grad_normed)
    grad_comp_slab = lax.dynamic_slice_in_dim(grad_stacked[:comp_len], column * slab, slab, 1)
    grad_tok_slab = lax.dynamic_slice_in_dim(grad_stacked[start_tok:], column * slab, slab, 1)
    grad_x = lax.dynamic_slice_in_dim(grad_resid, column * slab, slab, 1) + grad_tok_slab
    grad_comp_low = grad_comp_slab.astype(jnp.bfloat16)
    grad_comp = contract_rows(old_rows, grad_comp_low)
    grad_gains = jnp.stack([grad_gain_one, grad_gain_two], axis=0)
    comp_part, query_part, key_part, value_part, up_part = (
        lax.psum_scatter(grad_comp, "row", scatter_dimension=0, tiled=True),
        lax.psum_scatter(grad_query, "row", scatter_dimension=0, tiled=True),
        lax.psum_scatter(grad_key, "row", scatter_dimension=0, tiled=True),
        lax.psum_scatter(grad_value, "row", scatter_dimension=0, tiled=True),
        lax.psum_scatter(grad_up, "row", scatter_dimension=0, tiled=True),
    )
    proj_part, down_part, gains_part = (
        lax.psum_scatter(grad_proj, "row", scatter_dimension=1, tiled=True),
        lax.psum_scatter(grad_down, "row", scatter_dimension=1, tiled=True),
        lax.psum_scatter(grad_gains, "row", scatter_dimension=1, tiled=True),
    )
    return (
        layer_out,
        grad_x,
        gains_part,
        comp_part,
        query_part,
        key_part,
        value_part,
        proj_part,
        up_part,
        down_part,
    )


def solution(mesh):
    in_specs = (
        P("row", "col"),
        P("row", "col"),
        P("row", "col"),
        P("row", None),
        P(None, "row"),
        P("row", "col"),
        P("row", "col"),
        P("row", "col"),
        P("row", "col"),
        P("col", "row"),
        P("row", "col"),
        P("col", "row"),
        P("row", "col"),
    )
    out_specs = (
        P("row", "col"),
        P("row", "col"),
        P(None, "row"),
        P("row", "col"),
        P("row", "col"),
        P("row", "col"),
        P("row", "col"),
        P("col", "row"),
        P("row", "col"),
        P("col", "row"),
    )
    return jax.shard_map(
        on_device, mesh=mesh, in_specs=in_specs, out_specs=out_specs, check_vma=False
    )
```

profile of v0, /device:TPU:0, one launch (start us, length us, event | category | flops | bytes accessed | tf_op | source)
XLA Modules:
  0.0 1541.5 jit_solution(4942058512463735601)
XLA Ops:
  10.1 46.2 %all-gather.11.cloned.1.call-done = bf16[1536,1024]{1,0:T(8,128)(2,1)} async-done(((bf16[1536,256]{1,0:T(8,128)(2,1)}), bf16[1536,1024]{1,0:T(8,128)(2,1)}) %all-gather.11.cloned.1.call-update) | async-done | bytes 3145744 | tf_op jit(solution)/shard_map/all_gather | solution.py:46
  60.6 22.7 %all-gather.13.cloned.1.call-done = bf16[3072,256]{1,0:T(8,128)(2,1)} async-done(((bf16[384,256]{1,0:T(8,128)(2,1)}), bf16[3072,256]{1,0:T(8,128)(2,1)}) %all-gather.13.cloned.1.call-update) | async-done | bytes 1572880 | tf_op jit(solution)/shard_map/all_gather | solution.py:50
  98.6 15.8 %all_gather.45 = bf16[1024,256]{1,0:T(8,128)(2,1)} all-gather(bf16[128,256]{1,0:T(8,128)(2,1)S(1)} %copy-done.47), channel_id=1, replica_groups=mesh['row'=8,'col'=4] {'row'}, dimensions={0}, use_global_device_ids=true | all-gather | bytes 589824 | tf_op jit(solution)/shard_map/all_gather | solution.py:51
  114.4 15.8 %all_gather.46 = bf16[1024,256]{1,0:T(8,128)(2,1)} all-gather(bf16[128,256]{1,0:T(8,128)(2,1)S(1)} %copy-done.48), channel_id=1, replica_groups=mesh['row'=8,'col'=4] {'row'}, dimensions={0}, use_global_device_ids=true | all-gather | bytes 589824 | tf_op jit(solution)/shard_map/all_gather | solution.py:52
  130.2 15.8 %all_gather.47 = bf16[1024,256]{1,0:T(8,128)(2,1)} all-gather(bf16[128,256]{1,0:T(8,128)(2,1)S(1)} %copy-done.49), channel_id=1, replica_groups=mesh['row'=8,'col'=4] {'row'}, dimensions={0}, use_global_device_ids=true | all-gather | bytes 589824 | tf_op jit(solution)/shard_map/all_gather | solution.py:53
  146.1 15.2 all_gather.48
  164.8 28.6 %all-gather.15.cloned.1.call-done = bf16[512,1024]{1,0:T(8,128)(2,1)} async-done(((bf16[512,256]{1,0:T(8,128)(2,1)}), bf16[512,1024]{1,0:T(8,128)(2,1)}) %all-gather.15.cloned.1.call-update) | async-done | bytes 1048592 | tf_op jit(solution)/shard_map/all_gather | solution.py:75
  232.0 61.1 %while.30 = (s32[]{:T(128)}, bf16[4,512,2,128]{3,1,2,0:T(8,128)(2,1)}, f32[4,2,512,1]{2,1,3,0:T(2,128)S(1)}, f32[4,2,512,1]{2,1,3,0:T(2,128)S(1)}, s32[4,512]{1,...) while((s32[]{:T(128)}, ...), condition=%wide.region_5.6_spmd.clone, body=%wide.region_2.5_spmd.clone.sunk | while | flops 1653081088 | bytes 56447168 | solution.py:124
  314.3 160.6 %all-reduce.5.cloned.1.call-done = f32[2048,1024]{1,0:T(8,128)} async-done(((f32[2048,1024]{1,0:T(8,128)}), f32[2048,1024]{1,0:T(8,128)}) %all-reduce.5.cloned.1.call-update) | async-done | bytes 8388624 | tf_op jit(solution)/shard_map/psum | solution.py:126
  486.3 20.1 %all-gather.19.cloned.1.call-done = bf16[1024,1024]{1,0:T(8,128)(2,1)} async-done(((bf16[128,1024]{1,0:T(8,128)(2,1)}), bf16[1024,1024]{1,0:T(8,128)(2,1)}) %all-gather.19.cloned.1.call-update) | async-done | bytes 2097168 | tf_op jit(solution)/shard_map/all_gather | solution.py:54
  506.4 16.1 %fusion.50 = (bf16[2048,1024]{1,0:T(8,128)(2,1)S(1)}, f32[2048,1024]{1,0:T(8,128)}) fusion(f32[2048,1024]{1,0:T(8,128)} %fusion.78, bf16[2048,1024]{1,0:T(8,128)(2,1)} %multiply_convert_fusion.2, bf16[1024,1024]{1,0:T(8,128)(2,1)} %all-gather.19.cloned.1.call-done), kind=kOutput, calls=%fused_computation.73 | convolution fusion | flops 4336910336 | bytes 27262976 | tf_op jit(solution)/shard_map/dot_general | solution.py:129
  531.6 171.5 %all-reduce.9.cloned.1.call-done = f32[2048,1024]{1,0:T(8,128)} async-done(((f32[2048,1024]{1,0:T(8,128)}), f32[2048,1024]{1,0:T(8,128)}) %all-reduce.9.cloned.1.call-update) | async-done | bytes 8388624 | tf_op jit(solution)/shard_map/psum | solution.py:139
  726.2 122.1 %while.31 = (s32[]{:T(128)}, f32[3072,2,128]{0,2,1:T(8,128)S(1)}, f32[3072,2,128]{0,2,1:T(8,128)}, bf16[4,512,2,128]{3,1,2,0:T(8,128)(2,1)}, bf16[4,512,2,128]{3...) while((s32[]{:T(128)}, f32[3072,2,128]{0,2,1:T(8,128)S(1)}, ...), condition=%wide.region_15.16_spmd.clone, body=%wide.region_13.15_spmd.clone.sunk | while | flops 4066772992 | bytes 161038704 | solution.py:177
  887.5 227.9 %all-reduce.11.cloned.1.call-done = f32[3072,1024]{1,0:T(8,128)} async-done(((f32[3072,1024]{1,0:T(8,128)}), f32[3072,1024]{1,0:T(8,128)}) %all-reduce.11.cloned.1.call-update) | async-done | bytes 12582928 | tf_op jit(solution)/shard_map/psum | solution.py:193
  1171.6 12.3 fusion.74
  1206.9 15.3 all-reduce.7.cloned.1.call-done
  1232.0 23.9 %reduce-scatter.25.cloned.1.call-done = f32[128,2]{1,0:T(8,128)} async-done(((f32[1024,2]{1,0:T(8,128)}), f32[128,2]{1,0:T(8,128)}) %reduce-scatter.25.cloned.1.call-update) | async-done | bytes 1040
  1257.4 39.2 %reduce-scatter.11.cloned.1.call-done = f32[384,256]{0,1:T(8,128)} async-done(((f32[3072,256]{0,1:T(8,128)}), f32[384,256]{0,1:T(8,128)}) %reduce-scatter.11.cloned.1.call-update) | async-done | bytes 393232 | tf_op jit(solution)/shard_map/reduce_scatter | solution.py:203
  1298.6 50.2 %reduce-scatter.21.cloned.1.call-done = f32[128,1024]{1,0:T(8,128)} async-done(((f32[1024,1024]{1,0:T(8,128)}), f32[128,1024]{1,0:T(8,128)}) %reduce-scatter.21.cloned.1.call-update) | async-done | bytes 524304 | tf_op jit(solution)/shard_map/reduce_scatter | solution.py:207
  1348.7 51.1 %reduce-scatter.23.cloned.1.call-done = f32[1024,128]{1,0:T(8,128)} async-done(((f32[1024,1024]{1,0:T(8,128)}), f32[1024,128]{1,0:T(8,128)}) %reduce-scatter.23.cloned.1.call-update) | async-done | bytes 524304 | tf_op jit(solution)/shard_map/reduce_scatter | solution.py:211
  1399.8 33.8 %reduce-scatter.19.cloned.1.call-done = f32[256,128]{1,0:T(8,128)} async-done(((f32[256,1024]{1,0:T(8,128)}), f32[256,128]{1,0:T(8,128)}) %reduce-scatter.19.cloned.1.call-update) | async-done | bytes 131088 | tf_op jit(solution)/shard_map/reduce_scatter | solution.py:210
  1433.7 33.6 %reduce-scatter.13.cloned.1.call-done = f32[128,256]{1,0:T(8,128)} async-done(((f32[1024,256]{1,0:T(8,128)}), f32[128,256]{1,0:T(8,128)}) %reduce-scatter.13.cloned.1.call-update) | async-done | bytes 131088 | tf_op jit(solution)/shard_map/reduce_scatter | solution.py:204
  1467.2 33.8 %reduce-scatter.15.cloned.1.call-done = f32[128,256]{1,0:T(8,128)} async-done(((f32[1024,256]{1,0:T(8,128)}), f32[128,256]{1,0:T(8,128)}) %reduce-scatter.15.cloned.1.call-update) | async-done | bytes 131088 | tf_op jit(solution)/shard_map/reduce_scatter | solution.py:205
  1501.0 33.5 %reduce-scatter.17.cloned.1.call-done = f32[128,256]{1,0:T(8,128)} async-done(((f32[1024,256]{1,0:T(8,128)}), f32[128,256]{1,0:T(8,128)}) %reduce-scatter.17.cloned.1.call-update) | async-done | bytes 131088 | tf_op jit(solution)/shard_map/reduce_scatter | solution.py:206
  (355 shorter events, 441.8 us)
Async XLA Ops:
  7.2 49.1 %all-gather.11.cloned.1.call-start = ((), (), s32[]{:S(2)}) async-start(), calls=%async_computation.9 | async-start | bytes 3932160 | tf_op jit(solution)/shard_map/all_gather | solution.py:46
  8.0 75.3 %all-gather.13.cloned.1.call-start = ((), (), s32[]{:S(2)}) async-start(), calls=%async_computation.10 | async-start | bytes 1769472 | tf_op jit(solution)/shard_map/all_gather | solution.py:50
  8.7 152.6 %all-gather.17.cloned.1.call-start = ((), (), s32[]{:S(2)}) async-start(), calls=%async_computation.12 | async-start | bytes 1310720 | tf_op jit(solution)/shard_map/all_gather | solution.py:45
  9.5 155.3 %all-gather.9.cloned.1.call-start = ((), (), s32[]{:S(2)}) async-start(), calls=%async_computation.8 | async-start | bytes 5242880 | tf_op jit(solution)/shard_map/all_gather | solution.py:44
  10.0 183.4 %all-gather.15.cloned.1.call-start = ((), (), s32[]{:S(2)}) async-start(), calls=%async_computation.11 | async-start | bytes 1310720 | tf_op jit(solution)/shard_map/all_gather | solution.py:75
  86.4 217.2 %all-gather.21.cloned.1.call-start = ((), (), s32[]{:S(2)}) async-start(), calls=%async_computation.15 | async-start | bytes 2359296 | tf_op jit(solution)/shard_map/all_gather | solution.py:58
  86.9 216.6 %all-gather.23.cloned.1.call-start = ((), (), s32[]{:S(2)}) async-start(), calls=%async_computation.17 | async-start | bytes 5242880 | tf_op jit(solution)/shard_map/all_gather | solution.py:47
  87.7 387.2 %all-reduce.5.cloned.1.call-start = ((), (), s32[]{:S(2)}) async-start(), calls=%async_computation.13 | async-start | bytes 16777216 | tf_op jit(solution)/shard_map/psum | solution.py:126
  302.8 203.6 %all-gather.19.cloned.1.call-start = ((), (), s32[]{:S(2)}) async-start(), calls=%async_computation.14 | async-start | bytes 2359296 | tf_op jit(solution)/shard_map/all_gather | solution.py:54
  303.5 399.6 %all-reduce.9.cloned.1.call-start = ((), (), s32[]{:S(2)}) async-start(), calls=%async_computation.18 | async-start | bytes 16777216 | tf_op jit(solution)/shard_map/psum | solution.py:139
  531.5 583.9 %all-reduce.11.cloned.1.call-start = ((), (), s32[]{:S(2)}) async-start(), calls=%async_computation.19 | async-start | bytes 25165824 | tf_op jit(solution)/shard_map/psum | solution.py:193
  875.3 346.9 %all-reduce.7.cloned.1.call-start = ((), (), s32[]{:S(2)}) async-start(), calls=%async_computation.16 | async-start | bytes 8388608 | tf_op jit(solution)/shard_map/psum | solution.py:132
  875.6 239.9 %copy-start.13 = (bf16[512,1024]{1,0:T(8,128)(2,1)S(1)}, bf16[512,1024]{1,0:T(8,128)(2,1)}, u32[]{:S(2)}) copy-start(bf16[512,1024]{1,0:T(8,128)(2,1)} %all-gather.17.cloned.1.call-done) | copy-start | bytes 3145732
  875.6 239.9 %copy-start.15 = (bf16[512,1024]{1,0:T(8,128)(2,1)S(1)}, bf16[512,1024]{1,0:T(8,128)(2,1)}, u32[]{:S(2)}) copy-start(bf16[512,1024]{1,0:T(8,128)(2,1)} %all-gather.15.cloned.1.call-done) | copy-start | bytes 3145732
  875.6 239.9 %copy-start.40 = (f32[3072]{0:T(1024)S(1)}, f32[3072]{0:T(1024)}, u32[]{:S(2)}) copy-start(f32[3072]{0:T(1024)} %copy-done.39) | copy-start | bytes 36868
  875.6 239.9 %copy-start.46 = (f32[1,1024]{1,0:T(1,128)S(1)}, f32[1,1024]{1,0:T(1,128)}, u32[]{:S(2)}) copy-start(f32[1,1024]{1,0:T(1,128)} %copy-done.45) | copy-start | bytes 12292
  887.5 368.5 %reduce-scatter.25.cloned.1.call-start = ((), (), s32[]{:S(2)}) async-start(), calls=%async_computation.27 | async-start | bytes 589824
  1156.4 140.2 %reduce-scatter.11.cloned.1.call-start = ((), (), s32[]{:S(2)}) async-start(), calls=%async_computation.20 | async-start | bytes 3538944 | tf_op jit(solution)/shard_map/reduce_scatter | solution.py:203
  1161.1 187.7 %reduce-scatter.21.cloned.1.call-start = ((), (), s32[]{:S(2)}) async-start(), calls=%async_computation.25 | async-start | bytes 4718592 | tf_op jit(solution)/shard_map/reduce_scatter | solution.py:207
  1171.6 228.3 %reduce-scatter.23.cloned.1.call-start = ((), (), s32[]{:S(2)}) async-start(), calls=%async_computation.26 | async-start | bytes 4718592 | tf_op jit(solution)/shard_map/reduce_scatter | solution.py:211
  1183.9 249.7 %reduce-scatter.19.cloned.1.call-start = ((), (), s32[]{:S(2)}) async-start(), calls=%async_computation.24 | async-start | bytes 1179648 | tf_op jit(solution)/shard_map/reduce_scatter | solution.py:210
  1189.6 277.6 %reduce-scatter.13.cloned.1.call-start = ((), (), s32[]{:S(2)}) async-start(), calls=%async_computation.21 | async-start | bytes 1179648 | tf_op jit(solution)/shard_map/reduce_scatter | solution.py:204
  1194.6 306.4 %reduce-scatter.15.cloned.1.call-start = ((), (), s32[]{:S(2)}) async-start(), calls=%async_computation.22 | async-start | bytes 1179648 | tf_op jit(solution)/shard_map/reduce_scatter | solution.py:205
  1201.2 333.3 %reduce-scatter.17.cloned.1.call-start = ((), (), s32[]{:S(2)}) async-start(), calls=%async_computation.23 | async-start | bytes 1179648 | tf_op jit(solution)/shard_map/reduce_scatter | solution.py:206
  (78 other events, 1711.4 us)
Sparse Core Ops, SparseCore 0:
  9.8 46.4 all-gather.10
  58.0 25.2 all-gather.12
  85.1 25.4 all-gather.16
  112.3 52.4 all-gather.8
  167.0 26.3 all-gather.14
  194.9 30.5 all-gather.20
  227.3 51.4 all-gather.22
  302.9 171.9 all-reduce.4
  476.5 29.8 all-gather.18
  531.6 171.4 all-reduce.8
  875.4 239.9 all-reduce.10
  1118.6 103.6 all-reduce.6
  1224.5 31.3 reduce-scatter.24
  1258.1 38.5 reduce-scatter.10
  1299.4 49.3 reduce-scatter.20
  1351.4 48.3 reduce-scatter.22
  1402.5 31.0 reduce-scatter.18
  1436.4 30.8 reduce-scatter.12
  1470.1 30.8 reduce-scatter.14
  1503.7 30.7 reduce-scatter.16
where the time goes:
time: 1550 us; the launch traced here: 1540 us
  waiting for transfers between devices  1000 us (65%)
  matrix products  250 us (16%)
  other arithmetic  142 us (9%)
  blocking collectives  72.7 us (5%)
  local copies, waits for them, and re-layouts  58.5 us (4%)
    psum x1, waiting for transfers between devices, on_device(): grad_normed = lax.psum(partial_rows, 'col')  228 us
    psum x1, waiting for transfers between devices, on_device(): grad_hidden = lax.psum(contract_cols(grad_upper, up_full), 'col')  172 us
    psum x1, waiting for transfers between devices, on_device(): lax.psum(jnp.dot(mixed, proj_full, preferred_element_type=jnp.float32), '...  161 us
    reduce_scatter x1, waiting for transfers between devices, on_device(): lax.psum_scatter(grad_down, 'row', scatter_dimension=1, tiled=True)  51.1 us
    reduce_scatter x1, waiting for transfers between devices, on_device(): lax.psum_scatter(grad_up, 'row', scatter_dimension=0, tiled=True)  50.2 us
    dot_general x8, matrix products, masked_scores(): jnp.einsum('qhd,khd->hqk', query_block, key_heads, preferred_element_type...  49.4 us
    dot_general x7, matrix products, contract_rows(): lax.dot_general(left, right, (((0,), (0,)), ((), ())), preferred_element_...  49.2 us
    all_gather x1, waiting for transfers between devices, on_device(): lax.all_gather(old_memory, 'col', axis=1, tiled=True)  46.2 us
  transfers between devices with their start and end apart: 20, of which 17 were waited for; matrix products, arithmetic and copies ran while one was open for 15% of the time, Pallas kernels for 0%

commit v1 on v0

--- a/solution.py
+++ b/solution.py
@@ -190,7 +190,11 @@
     partial_rows = jnp.concatenate(
         [back_keys[:start_tok], back_keys[start_tok:] + back_queries], axis=0
     )
-    grad_normed = lax.psum(partial_rows, "col")
+    grad_normed = partial_rows
+    for hop in (1, 2):
+        grad_normed = grad_normed + lax.ppermute(
+            grad_normed, "col", [(dev, dev ^ hop) for dev in range(4)]
+        )
     _, first_pull = jax.vjp(normalize, stacked, gain_one)
     grad_stacked, grad_gain_one = first_pull(grad_normed)
     grad_comp_slab = lax.dynamic_slice_in_dim(grad_stacked[:comp_len], column * slab, slab, 1)

time: 1550 us -> 1860 us (1.20)
  waiting for transfers between devices: 1000 us -> 1300 us
    ppermute x0 -> x2, waiting for transfers between devices: none -> 596 us  [on_device(): lax.ppermute(grad_normed, 'col', [(dev, dev ^ hop) for dev in range(4)])]
    psum x1 -> x0, waiting for transfers between devices: 228 us -> none  [on_device(): grad_normed = lax.psum(partial_rows, 'col')]
    reduce_scatter x1, waiting for transfers between devices: 39.2 us -> 12.2 us  [on_device(): lax.psum_scatter(grad_comp, 'row', scatter_dimension=0, tiled=True)]
    unnamed x21 -> x20, waiting for transfers between devices: 28.6 us -> 4.68 us
  transfers between devices with their start and end apart: 20 -> 21, of which waited for: 17 -> 16; matrix products, arithmetic and copies ran while one was open for 15% -> 13% of each run, Pallas kernels for 0% -> 0%
where the time goes in v1:
time: 1860 us
  waiting for transfers between devices  1300 us (70%)
  matrix products  248 us (13%)
  other arithmetic  160 us (9%)
  blocking collectives  72.7 us (4%)
  local copies, waits for them, and re-layouts  54.8 us (3%)
    ppermute x2, waiting for transfers between devices, on_device(): lax.ppermute(grad_normed, 'col', [(dev, dev ^ hop) for dev in range(4)])  596 us
    psum x1, waiting for transfers between devices, on_device(): grad_hidden = lax.psum(contract_cols(grad_upper, up_full), 'col')  172 us
    psum x1, waiting for transfers between devices, on_device(): lax.psum(jnp.dot(mixed, proj_full, preferred_element_type=jnp.float32), '...  161 us
    reduce_scatter x1, waiting for transfers between devices, on_device(): lax.psum_scatter(grad_down, 'row', scatter_dimension=1, tiled=True)  51.1 us
    reduce_scatter x1, waiting for transfers between devices, on_device(): lax.psum_scatter(grad_up, 'row', scatter_dimension=0, tiled=True)  50 us
    dot_general x8, matrix products, masked_scores(): jnp.einsum('qhd,khd->hqk', query_block, key_heads, preferred_element_type...  49.3 us
    dot_general x7, matrix products, contract_rows(): lax.dot_general(left, right, (((0,), (0,)), ((), ())), preferred_element_...  48.2 us
    all_gather x1, waiting for transfers between devices, on_device(): lax.all_gather(old_memory, 'col', axis=1, tiled=True)  46.2 us
  transfers between devices with their start and end apart: 21, of which 16 were waited for; matrix products, arithmetic and copies ran while one was open for 13% of the time, Pallas kernels for 0%

profile of v1, /device:TPU:0, one launch (start us, length us, event | category | flops | bytes accessed | tf_op | source)
XLA Modules:
  0.0 1858.2 jit_solution(1335826131025404506)
XLA Ops:
  10.1 46.2 %all-gather.11.cloned.1.call-done = bf16[1536,1024]{1,0:T(8,128)(2,1)} async-done(((bf16[1536,256]{1,0:T(8,128)(2,1)}), bf16[1536,1024]{1,0:T(8,128)(2,1)}) %all-gather.11.cloned.1.call-update) | async-done | bytes 3145744 | tf_op jit(solution)/shard_map/all_gather | solution.py:46
  60.6 22.7 %all-gather.13.cloned.1.call-done = bf16[3072,256]{1,0:T(8,128)(2,1)} async-done(((bf16[384,256]{1,0:T(8,128)(2,1)}), bf16[3072,256]{1,0:T(8,128)(2,1)}) %all-gather.13.cloned.1.call-update) | async-done | bytes 1572880 | tf_op jit(solution)/shard_map/all_gather | solution.py:50
  98.6 15.8 all_gather.45
  114.4 15.8 all_gather.46
  130.2 15.8 all_gather.47
  146.1 15.2 all_gather.48
  164.8 28.6 %all-gather.15.cloned.1.call-done = bf16[512,1024]{1,0:T(8,128)(2,1)} async-done(((bf16[512,256]{1,0:T(8,128)(2,1)}), bf16[512,1024]{1,0:T(8,128)(2,1)}) %all-gather.15.cloned.1.call-update) | async-done | bytes 1048592 | tf_op jit(solution)/shard_map/all_gather | solution.py:75
  232.0 61.1 %while.30 = (s32[]{:T(128)}, bf16[4,512,2,128]{3,1,2,0:T(8,128)(2,1)}, f32[4,2,512,1]{2,1,3,0:T(2,128)S(1)}, f32[4,2,512,1]{2,1,3,0:T(2,128)S(1)}, s32[4,512]{1,...) while((s32[]{:T(128)}, ...), condition=%wide.region_5.6_spmd.clone, body=%wide.region_2.5_spmd.clone.sunk | while | flops 1653081088 | bytes 56447168 | solution.py:124
  314.4 160.5 %all-reduce.4.cloned.1.call-done = f32[2048,1024]{1,0:T(8,128)} async-done(((f32[2048,1024]{1,0:T(8,128)}), f32[2048,1024]{1,0:T(8,128)}) %all-reduce.4.cloned.1.call-update) | async-done | bytes 8388624 | tf_op jit(solution)/shard_map/psum | solution.py:126
  486.3 20.1 %all-gather.19.cloned.1.call-done = bf16[1024,1024]{1,0:T(8,128)(2,1)} async-done(((bf16[128,1024]{1,0:T(8,128)(2,1)}), bf16[1024,1024]{1,0:T(8,128)(2,1)}) %all-gather.19.cloned.1.call-update) | async-done | bytes 2097168 | tf_op jit(solution)/shard_map/all_gather | solution.py:54
  506.4 16.0 fusion.50
  531.4 171.5 %all-reduce.8.cloned.1.call-done = f32[2048,1024]{1,0:T(8,128)} async-done(((f32[2048,1024]{1,0:T(8,128)}), f32[2048,1024]{1,0:T(8,128)}) %all-reduce.8.cloned.1.call-update) | async-done | bytes 8388624 | tf_op jit(solution)/shard_map/psum | solution.py:139
  726.0 122.1 %while.31 = (s32[]{:T(128)}, f32[3072,2,128]{0,2,1:T(8,128)S(1)}, f32[3072,2,128]{0,2,1:T(8,128)}, bf16[4,512,2,128]{3,1,2,0:T(8,128)(2,1)}, bf16[4,512,2,128]{3...) while((s32[]{:T(128)}, f32[3072,2,128]{0,2,1:T(8,128)S(1)}, ...), condition=%wide.region_15.16_spmd.clone, body=%wide.region_13.15_spmd.clone.sunk | while | flops 4066772992 | bytes 161038704 | solution.py:177
  876.6 270.6 %collective-permute-done = f32[3072,1024]{1,0:T(8,128)S(1)} collective-permute-done((f32[3072,1024]{1,0:T(8,128)}, f32[3072,1024]{1,0:T(8,128)S(1)}, u32[]{:S(2)}, u32[]{:S(2)}) %collective-permute-start) | collective-permute-done | bytes 12582944 | tf_op jit(solution)/shard_map/ppermute | solution.py:195
  1170.7 325.7 %collective-permute-done.1 = f32[3072,1024]{1,0:T(8,128)} collective-permute-done((f32[3072,1024]{1,0:T(8,128)}, f32[3072,1024]{1,0:T(8,128)}, u32[]{:S(2)}, u32[]{:S(2)}) %collective-permute-start.1) | collective-permute-done | bytes 12582944 | tf_op jit(solution)/shard_map/ppermute | solution.py:195
  1496.4 13.3 fusion.41
  1510.7 17.2 fusion.76
  1601.6 12.2 reduce-scatter.11.cloned.1.call-done
  1615.8 50.0 %reduce-scatter.21.cloned.1.call-done = f32[128,1024]{1,0:T(8,128)} async-done(((f32[1024,1024]{1,0:T(8,128)}), f32[128,1024]{1,0:T(8,128)}) %reduce-scatter.21.cloned.1.call-update) | async-done | bytes 524304 | tf_op jit(solution)/shard_map/reduce_scatter | solution.py:211
  1665.8 51.1 %reduce-scatter.23.cloned.1.call-done = f32[1024,128]{1,0:T(8,128)} async-done(((f32[1024,1024]{1,0:T(8,128)}), f32[1024,128]{1,0:T(8,128)}) %reduce-scatter.23.cloned.1.call-update) | async-done | bytes 524304 | tf_op jit(solution)/shard_map/reduce_scatter | solution.py:215
  1716.9 33.8 %reduce-scatter.19.cloned.1.call-done = f32[256,128]{1,0:T(8,128)} async-done(((f32[256,1024]{1,0:T(8,128)}), f32[256,128]{1,0:T(8,128)}) %reduce-scatter.19.cloned.1.call-update) | async-done | bytes 131088 | tf_op jit(solution)/shard_map/reduce_scatter | solution.py:214
  1750.7 33.7 %reduce-scatter.13.cloned.1.call-done = f32[128,256]{1,0:T(8,128)} async-done(((f32[1024,256]{1,0:T(8,128)}), f32[128,256]{1,0:T(8,128)}) %reduce-scatter.13.cloned.1.call-update) | async-done | bytes 131088 | tf_op jit(solution)/shard_map/reduce_scatter | solution.py:208
  1784.4 33.5 %reduce-scatter.15.cloned.1.call-done = f32[128,256]{1,0:T(8,128)} async-done(((f32[1024,256]{1,0:T(8,128)}), f32[128,256]{1,0:T(8,128)}) %reduce-scatter.15.cloned.1.call-update) | async-done | bytes 131088 | tf_op jit(solution)/shard_map/reduce_scatter | solution.py:209
  1817.9 33.6 %reduce-scatter.17.cloned.1.call-done = f32[128,256]{1,0:T(8,128)} async-done(((f32[1024,256]{1,0:T(8,128)}), f32[128,256]{1,0:T(8,128)}) %reduce-scatter.17.cloned.1.call-update) | async-done | bytes 131088 | tf_op jit(solution)/shard_map/reduce_scatter | solution.py:210
  (353 shorter events, 438.9 us)
Async XLA Ops:
  7.2 49.1 %all-gather.11.cloned.1.call-start = ((), (), s32[]{:S(2)}) async-start(), calls=%async_computation.9 | async-start | bytes 3932160 | tf_op jit(solution)/shard_map/all_gather | solution.py:46
  8.0 75.3 %all-gather.13.cloned.1.call-start = ((), (), s32[]{:S(2)}) async-start(), calls=%async_computation.10 | async-start | bytes 1769472 | tf_op jit(solution)/shard_map/all_gather | solution.py:50
  8.7 152.6 %all-gather.17.cloned.1.call-start = ((), (), s32[]{:S(2)}) async-start(), calls=%async_computation.12 | async-start | bytes 1310720 | tf_op jit(solution)/shard_map/all_gather | solution.py:45
  9.5 155.3 %all-gather.9.cloned.1.call-start = ((), (), s32[]{:S(2)}) async-start(), calls=%async_computation.8 | async-start | bytes 5242880 | tf_op jit(solution)/shard_map/all_gather | solution.py:44
  10.0 183.4 %all-gather.15.cloned.1.call-start = ((), (), s32[]{:S(2)}) async-start(), calls=%async_computation.11 | async-start | bytes 1310720 | tf_op jit(solution)/shard_map/all_gather | solution.py:75
  86.4 217.2 %all-gather.21.cloned.1.call-start = ((), (), s32[]{:S(2)}) async-start(), calls=%async_computation.15 | async-start | bytes 2359296 | tf_op jit(solution)/shard_map/all_gather | solution.py:58
  86.9 216.7 %all-gather.23.cloned.1.call-start = ((), (), s32[]{:S(2)}) async-start(), calls=%async_computation.17 | async-start | bytes 5242880 | tf_op jit(solution)/shard_map/all_gather | solution.py:47
  87.7 387.2 %all-reduce.4.cloned.1.call-start = ((), (), s32[]{:S(2)}) async-start(), calls=%async_computation.13 | async-start | bytes 16777216 | tf_op jit(solution)/shard_map/psum | solution.py:126
  302.8 203.6 %all-gather.19.cloned.1.call-start = ((), (), s32[]{:S(2)}) async-start(), calls=%async_computation.14 | async-start | bytes 2359296 | tf_op jit(solution)/shard_map/all_gather | solution.py:54
  303.5 399.4 %all-reduce.8.cloned.1.call-start = ((), (), s32[]{:S(2)}) async-start(), calls=%async_computation.18 | async-start | bytes 16777216 | tf_op jit(solution)/shard_map/psum | solution.py:139
  531.3 1058.9 %all-reduce.6.cloned.1.call-start = ((), (), s32[]{:S(2)}) async-start(), calls=%async_computation.16 | async-start | bytes 8388608 | tf_op jit(solution)/shard_map/psum | solution.py:132
  875.1 272.1 %collective-permute-start = (f32[3072,1024]{1,0:T(8,128)}, f32[3072,1024]{1,0:T(8,128)S(1)}, u32[]{:S(2)}, u32[]{:S(2)}) collective-permute-start(f32[3072,1024]{1,0:T(8,128)} %pad_maximum_fusion), channel_id=1, source_target_pairs={{0,1},{1,0},{2,3},{3,2},{4,5},{5,4},{6,7},{7,6},{8,9},{9,8},{10,11... | collective-permute-start | bytes 37748744 | tf_op jit(solution)/shard_map/ppermute | solution.py:195
  1157.5 338.8 %collective-permute-start.1 = (f32[3072,1024]{1,0:T(8,128)}, f32[3072,1024]{1,0:T(8,128)}, u32[]{:S(2)}, u32[]{:S(2)}) collective-permute-start(f32[3072,1024]{1,0:T(8,128)} %fusion.74), channel_id=1, source_target_pairs={{0,2},{1,3},{2,0},{3,1},{4,6},{5,7},{6,4},{7,5},{8,10},{9,11},{10,... | collective-permute-start | bytes 37748744 | tf_op jit(solution)/shard_map/ppermute | solution.py:195
  1158.9 337.5 %copy-start.48 = (f32[1,1024]{1,0:T(1,128)S(1)}, f32[1,1024]{1,0:T(1,128)}, u32[]{:S(2)}) copy-start(f32[1,1024]{1,0:T(1,128)} %copy-done.47) | copy-start | bytes 12292
  1170.6 339.1 %copy-start.51 = (f32[1024]{0:T(1024)S(1)}, f32[1024]{0:T(1024)}, u32[]{:S(2)}) copy-start(f32[1024]{0:T(1024)} %get-tuple-element.316) | copy-start | bytes 12292
  1170.6 340.1 %copy-start.42 = (f32[3072]{0:T(1024)S(1)}, f32[3072]{0:T(1024)}, u32[]{:S(2)}) copy-start(f32[3072]{0:T(1024)} %copy-done.41) | copy-start | bytes 36868
  1170.6 429.6 %reduce-scatter.25.cloned.1.call-start = ((), (), s32[]{:S(2)}) async-start(), calls=%async_computation.26 | async-start | bytes 589824
  1540.9 73.0 %reduce-scatter.11.cloned.1.call-start = ((), (), s32[]{:S(2)}) async-start(), calls=%async_computation.19 | async-start | bytes 3538944 | tf_op jit(solution)/shard_map/reduce_scatter | solution.py:207
  1545.1 120.7 %reduce-scatter.21.cloned.1.call-start = ((), (), s32[]{:S(2)}) async-start(), calls=%async_computation.24 | async-start | bytes 4718592 | tf_op jit(solution)/shard_map/reduce_scatter | solution.py:211
  1555.3 161.6 %reduce-scatter.23.cloned.1.call-start = ((), (), s32[]{:S(2)}) async-start(), calls=%async_computation.25 | async-start | bytes 4718592 | tf_op jit(solution)/shard_map/reduce_scatter | solution.py:215
  1567.5 183.2 %reduce-scatter.19.cloned.1.call-start = ((), (), s32[]{:S(2)}) async-start(), calls=%async_computation.23 | async-start | bytes 1179648 | tf_op jit(solution)/shard_map/reduce_scatter | solution.py:214
  1573.2 211.2 %reduce-scatter.13.cloned.1.call-start = ((), (), s32[]{:S(2)}) async-start(), calls=%async_computation.20 | async-start | bytes 1179648 | tf_op jit(solution)/shard_map/reduce_scatter | solution.py:208
  1578.3 239.6 %reduce-scatter.15.cloned.1.call-start = ((), (), s32[]{:S(2)}) async-start(), calls=%async_computation.21 | async-start | bytes 1179648 | tf_op jit(solution)/shard_map/reduce_scatter | solution.py:209
  1584.4 267.1 %reduce-scatter.17.cloned.1.call-start = ((), (), s32[]{:S(2)}) async-start(), calls=%async_computation.22 | async-start | bytes 1179648 | tf_op jit(solution)/shard_map/reduce_scatter | solution.py:210
  (77 other events, 2559.4 us)
Sparse Core Ops, SparseCore 0:
  9.8 46.4 all-gather.10
  58.0 25.2 all-gather.12
  85.1 25.4 all-gather.16
  112.3 52.4 all-gather.8
  167.0 26.3 all-gather.14
  194.9 30.5 all-gather.20
  227.3 51.4 all-gather.22
  302.9 171.9 all-reduce.3
  476.5 29.8 all-gather.18
  531.5 171.4 all-reduce.7
  1170.7 171.4 all-reduce.5
  1541.0 31.9 reduce-scatter.24
  1575.3 38.5 reduce-scatter.10
  1616.6 49.1 reduce-scatter.20
  1668.5 48.3 reduce-scatter.22
  1719.6 31.0 reduce-scatter.18
  1753.4 30.9 reduce-scatter.12
  1787.1 30.7 reduce-scatter.14
  1820.7 30.7 reduce-scatter.16
